TPU v7x, 128 devices: a whole 4x4x4 slice. The times are simulated.
128 devices in a mesh: seq: 16 (over x, z), exp: 8 (over y, core).
Axes of the slice: x: 4, y: 4, z: 4, core: 2. Of those that a mesh axis runs over, the one named last changes fastest.
Arguments:
- ssd_input: bfloat16 [8192, 2, 4096], P('seq', None, 'exp'), may hold values from -6 to 6
- ssd_gate: bfloat16 [8192, 2, 4096], P('seq', None, 'exp'), may hold values from -6 to 6
- state_write: bfloat16 [8192, 2, 1024], P('seq', None, 'exp'), may hold values from -2 to 2
- state_read: bfloat16 [8192, 2, 1024], P('seq', None, 'exp'), may hold values from -2 to 2
- step_size: float32 [64, 2, 8192], P('exp', None, 'seq'), may hold values from 0.02 to 0.1
- decay_log: float32 [64, 2, 8192], P('exp', None, 'seq'), may hold values from -0.78 to 0
- skip_gain: float32 [64], P('exp'), may hold values from 0.5 to 2
- norm_gain: float32 [4096], P('exp'), may hold values from 0.5 to 1.5
- w_out: bfloat16 [4096, 2048], P('exp'), may hold values from -0.09375 to 0.09375
- resid: bfloat16 [8192, 2, 2048], P(('seq', 'exp')), may hold values from -6 to 6
- moe_gain: float32 [2048], replicated, may hold values from 0.5 to 1.5
- w_gate: bfloat16 [16, 2048, 7168], P('seq', None, 'exp'), may hold values from -0.125 to 0.125
- w_up: bfloat16 [16, 2048, 7168], P('seq', None, 'exp'), may hold values from -0.125 to 0.125
- w_down: bfloat16 [16, 7168, 2048], P('seq', 'exp'), may hold values from -0.0625 to 0.0625
- routes: int32 [8192, 2, 2], P(('seq', 'exp')), may hold values from 0 to 15, all different within a row; in each aligned block of 128 rows (0 to 127, 128 to 255, ..., all dimensions but the last counted through in order) at most 17 rows name the same one
- gates: float32 [8192, 2, 2], P(('seq', 'exp')), may hold values from 0.2 to 1
- directions: float32 [4, 2048], replicated, may hold values from -6 to 6
Outputs:
- steered: bfloat16 [8192, 2, 2048], P(('seq', 'exp'))
Inputs may be any that keep to these rules, and one draw needn't show every extreme that they name: `routes`: in every aligned block of 128 rows, rows taken in the order position then sequence (the rows of one device), each expert is named by at most 17 picks, a bound that some block reaches; the two ids of a row differ.
All inputs are finite; a program needn't handle non-finite values.
Results may differ from a plain program's by a relative error of at most 0.023.
Values may be sent and summed in bfloat16 or wider, within the bound.
No kernel may reach another device: no remote copies, remote signals or barrier semaphores. Data moves between devices by JAX's collectives and lax.ppermute only.
A program may use at most 128 MiB of HBM per device.

v0:
```python
import jax
import jax.numpy as jnp
from jax import lax
from jax.sharding import PartitionSpec as P

D = 2048
HEADS = 64
HEAD_DIM = 64
STATE = 128
GROUPS = 8
BLOCK = 256


def shifted(block, axis, distance):
    devices = range(lax.axis_size(axis))
    route = [(i - distance, i) for i in devices if i - distance in devices]
    return lax.ppermute(block, axis, route)


def build_slots(tokens, chosen, experts, capacity):
    picks = chosen.reshape(-1)
    onehot = (picks[:, None] == jnp.arange(experts, dtype=jnp.int32)[None, :]).astype(jnp.int32)
    before = jnp.cumsum(onehot, axis=0) - onehot
    ranked = jnp.sum(before * onehot, axis=1)
    places = picks * capacity + ranked
    layout = jnp.arange(experts * capacity, dtype=jnp.int32)
    select = jnp.any(layout[:, None, None] == places.reshape(-1, 2)[None, :, :], axis=2).astype(
        jnp.bfloat16
    )
    buffer = jnp.dot(select, tokens, preferred_element_type=jnp.float32).astype(jnp.bfloat16)
    return (buffer, places)


def on_device(
    ssd_input,
    ssd_gate,
    state_write,
    state_read,
    step_size,
    decay_log,
    skip_gain,
    norm_gain,
    w_out,
    resid,
    moe_gain,
    w_gate,
    w_up,
    w_down,
    routes,
    gates,
    directions,
):
    length_dev, seqs, width_dev = ssd_input.shape
    heads_dev = decay_log.shape[0]
    per_group = HEADS // GROUPS
    groups_dev = heads_dev // per_group
    blocks = length_dev // BLOCK
    inputs = ssd_input.reshape(blocks, BLOCK, seqs, groups_dev, per_group, HEAD_DIM)
    writes = state_write.reshape(blocks, BLOCK, seqs, groups_dev, STATE)
    reads = state_read.reshape(blocks, BLOCK, seqs, groups_dev, STATE)

    def arrange(values):
        moved = jnp.transpose(values.reshape(heads_dev, seqs, blocks, BLOCK), (2, 1, 0, 3))
        return moved.reshape(blocks, seqs, groups_dev, per_group, BLOCK)

    decays = jnp.cumsum(arrange(decay_log), axis=-1)
    steps_in = arrange(step_size)
    scores = jnp.einsum("ctbgn,cubgn->cbgtu", reads, writes, preferred_element_type=jnp.float32)
    row_pos = lax.broadcasted_iota(jnp.int32, (BLOCK, BLOCK), 0)
    col_pos = lax.broadcasted_iota(jnp.int32, (BLOCK, BLOCK), 1)
    causal = row_pos >= col_pos
    spread = decays[..., :, None] - decays[..., None, :]
    kernel = (
        jnp.where(causal, jnp.exp(jnp.where(causal, spread, 0.0)), 0.0) * steps_in[..., None, :]
    )
    weights = (kernel * scores[:, :, :, None]).astype(jnp.bfloat16)
    within = jnp.einsum(
        "cbgitu,cubgip->ctbgip", weights, inputs, preferred_element_type=jnp.float32
    )
    to_end = jnp.exp(decays[..., -1:] - decays) * steps_in
    scaled = (inputs * jnp.transpose(to_end, (0, 4, 1, 2, 3))[..., None]).astype(jnp.bfloat16)
    contrib = jnp.einsum("cubgip,cubgn->cbgipn", scaled, writes, preferred_element_type=jnp.float32)
    through = jnp.exp(decays[..., -1])
    running = jnp.zeros(contrib.shape[1:], jnp.float32)
    carried = jnp.ones(through.shape[1:], jnp.float32)
    starts = []
    prefixes = []
    for index in range(blocks):
        starts.append(running)
        prefixes.append(carried)
        running = through[index][..., None, None] * running + contrib[index]
        carried = carried * through[index]

    def link(turn, state):
        return shifted(
            (carried[..., None, None] * state + running).astype(jnp.bfloat16), "seq", 1
        ).astype(jnp.float32)

    entering = lax.fori_loop(0, lax.axis_size("seq") - 1, link, jnp.zeros_like(running))
    begin = jnp.stack(starts) + jnp.stack(prefixes)[..., None, None] * entering[None]
    readout = jnp.einsum(
        "cbgipn,ctbgn->ctbgip", begin, reads.astype(jnp.float32), precision=lax.Precision.HIGHEST
    )
    across = jnp.transpose(jnp.exp(decays), (0, 4, 1, 2, 3))[..., None] * readout
    ssd_out = (within + across).reshape(length_dev, seqs, width_dev) + jnp.repeat(
        skip_gain, HEAD_DIM
    ) * ssd_input.astype(jnp.float32)
    gated = ssd_out * jax.nn.silu(ssd_gate.astype(jnp.float32))
    grouped = gated.reshape(length_dev, seqs, groups_dev, per_group * HEAD_DIM)
    factor = lax.rsqrt(jnp.mean(grouped * grouped, axis=-1, keepdims=True) + 1e-05)
    normed = ((grouped * factor).reshape(length_dev, seqs, width_dev) * norm_gain).astype(
        jnp.bfloat16
    )
    flat_normed = normed.reshape(length_dev * seqs, width_dev)
    columns = lax.axis_size("exp")
    rows_keep = length_dev * seqs // columns
    piece = flat_normed
    mixed = lax.psum_scatter(
        jnp.dot(piece, w_out, preferred_element_type=jnp.float32).astype(jnp.bfloat16),
        "exp",
        scatter_dimension=0,
        tiled=True,
    ).astype(jnp.float32)
    hidden_state = resid.reshape(rows_keep, D).astype(jnp.float32) + mixed
    scale = lax.rsqrt(jnp.mean(hidden_state * hidden_state, axis=-1, keepdims=True) + 1e-05)
    moe_in = (hidden_state * scale * moe_gain).astype(jnp.bfloat16)
    experts = lax.axis_size("seq")
    capacity = max(2, 2 * rows_keep * 17 // (16 * experts))
    chosen = routes.reshape(rows_keep, 2)
    hidden_units = w_gate.shape[2]
    all_tokens, all_routes = (
        lax.all_gather(moe_in, "exp", axis=0, tiled=True),
        lax.all_gather(chosen, "exp", axis=0, tiled=True),
    )
    buffers, all_places = jax.vmap(build_slots, in_axes=(0, 0, None, None))(
        all_tokens.reshape(columns, rows_keep, D),
        all_routes.reshape(columns, rows_keep, 2),
        experts,
        capacity,
    )
    places = lax.dynamic_index_in_dim(all_places, lax.axis_index("exp"), 0, keepdims=False)
    arrived = lax.all_to_all(
        buffers.reshape(columns, experts, capacity, D),
        "seq",
        split_axis=1,
        concat_axis=1,
        tiled=True,
    )
    rows = arrived.reshape(-1, D)
    gate_value = jnp.dot(rows, w_gate[0], preferred_element_type=jnp.float32)
    up_value = jnp.dot(rows, w_up[0], preferred_element_type=jnp.float32)
    hidden = (jax.nn.silu(gate_value) * up_value).astype(jnp.bfloat16)
    hidden_all = hidden.reshape(arrived.shape[:-1] + (hidden_units,))
    flat_hidden = hidden_all.reshape(-1, hidden_units)
    piece = flat_hidden
    summed = lax.psum_scatter(
        jnp.dot(piece, w_down[0], preferred_element_type=jnp.float32).astype(jnp.bfloat16),
        "exp",
        scatter_dimension=0,
        tiled=True,
    )
    returned = lax.all_to_all(
        summed.reshape(experts, capacity, D), "seq", split_axis=0, concat_axis=0, tiled=True
    )
    picked = (
        jnp.take(returned.reshape(experts * capacity, D), places, axis=0)
        .astype(jnp.float32)
        .reshape(rows_keep, 2, D)
    )
    combined = hidden_state + jnp.sum(gates.reshape(rows_keep, 2)[..., None] * picked, axis=1)
    for index in range(directions.shape[0]):
        direction = directions[index]
        along = jnp.dot(combined, direction, precision=lax.Precision.HIGHEST) / (
            jnp.sum(direction * direction) + 1e-06
        )
        combined = combined - along[:, None] * direction[None, :]
    return combined.astype(jnp.bfloat16).reshape(length_dev // columns, seqs, D)


def solution(mesh):
    in_specs = (
        P("seq", None, "exp"),
        P("seq", None, "exp"),
        P("seq", None, "exp"),
        P("seq", None, "exp"),
        P("exp", None, "seq"),
        P("exp", None, "seq"),
        P("exp"),
        P("exp"),
        P("exp", None),
        P(("seq", "exp"), None, None),
        P(),
        P("seq", None, "exp"),
        P("seq", None, "exp"),
        P("seq", "exp", None),
        P(("seq", "exp"), None, None),
        P(("seq", "exp"), None, None),
        P(),
    )
    out_specs = P(("seq", "exp"), None, None)
    return jax.shard_map(
        on_device, mesh=mesh, in_specs=in_specs, out_specs=out_specs, check_vma=False
    )
```

profile of v0, /device:TPU:0, one launch (start us, length us, event | category | flops | bytes accessed | tf_op | source)
XLA Modules:
  0.0 622.5 jit_solution(711076186211400162)
XLA Ops:
  23.8 170.2 %while.11 = (s32[]{:T(128)}, f32[2,1,8,64,128]{4,3,2,1,0:T(8,128)S(1)}, f32[2,1,8]{2,0,1:T(2,128)S(1)}, f32[2,1,8,64,128]{4,3,2,1,0:T(8,128)S(1)}, s32[]{:T(128)}, /*index=5*/s32[]{:T(128)}) while((s32[]{:T(128)}, f32[2,1,8,64,128]{4,3,2,1,0:T(8,128)S(1)}, f32[2,1,8]{2,0,1:T(2,128)S(1)}, f32[2,1,8,64,128]{4,3,2,1,0:T(8,128)S(1)}, ...), condition=%wide.region_3.4_spmd.clone, body=%wide.region_2.3_spmd.clone.sunk | while | flops 655363 | bytes 3145911 | solution.py:99
  28.5 5.8 collective-permute-done
  35.3 4.3 collective-permute-start
  39.5 5.0 collective-permute-done
  45.4 4.3 collective-permute-start
  49.7 4.2 collective-permute-done
  54.8 4.3 collective-permute-start
  59.1 4.2 collective-permute-done
  64.1 4.3 collective-permute-start
  68.4 4.2 collective-permute-done
  73.5 5.5 collective-permute-start
  78.9 4.2 collective-permute-done
  84.0 6.4 %collective-permute-start = (bf16[2,1,8,64,128]{4,3,2,1,0:T(8,128)(2,1)}, bf16[2,1,8,64,128]{4,3,2,1,0:T(8,128)(2,1)S(1)}, u32[]{:S(2)}, u32[]{:S(2)}) collective-permute-start(bf16[2,1,8,64,128]{4,3,2,1,0:T(8,128)(2,1)} %fusion.85), channel_id=1, source_target_pairs={{0,8},{8,16},{16,24},{24,32},{32,40},{40,48},{48,56},{56,64},{64,7... | collective-permute-start | bytes 786440 | tf_op jit(solution)/shard_map/while/body/eval_jaxpr/ppermute | solution.py:17
  90.4 4.2 collective-permute-done
  95.5 6.4 %collective-permute-start = (bf16[2,1,8,64,128]{4,3,2,1,0:T(8,128)(2,1)}, bf16[2,1,8,64,128]{4,3,2,1,0:T(8,128)(2,1)S(1)}, u32[]{:S(2)}, u32[]{:S(2)}) collective-permute-start(bf16[2,1,8,64,128]{4,3,2,1,0:T(8,128)(2,1)} %fusion.85), channel_id=1, source_target_pairs={{0,8},{8,16},{16,24},{24,32},{32,40},{40,48},{48,56},{56,64},{64,7... | collective-permute-start | bytes 786440 | tf_op jit(solution)/shard_map/while/body/eval_jaxpr/ppermute | solution.py:17
  101.9 4.3 collective-permute-done
  107.0 6.7 %collective-permute-start = (bf16[2,1,8,64,128]{4,3,2,1,0:T(8,128)(2,1)}, bf16[2,1,8,64,128]{4,3,2,1,0:T(8,128)(2,1)S(1)}, u32[]{:S(2)}, u32[]{:S(2)}) collective-permute-start(bf16[2,1,8,64,128]{4,3,2,1,0:T(8,128)(2,1)} %fusion.85), channel_id=1, source_target_pairs={{0,8},{8,16},{16,24},{24,32},{32,40},{40,48},{48,56},{56,64},{64,7... | collective-permute-start | bytes 786440 | tf_op jit(solution)/shard_map/while/body/eval_jaxpr/ppermute | solution.py:17
  113.7 5.3 collective-permute-done
  120.0 7.0 %collective-permute-start = (bf16[2,1,8,64,128]{4,3,2,1,0:T(8,128)(2,1)}, bf16[2,1,8,64,128]{4,3,2,1,0:T(8,128)(2,1)S(1)}, u32[]{:S(2)}, u32[]{:S(2)}) collective-permute-start(bf16[2,1,8,64,128]{4,3,2,1,0:T(8,128)(2,1)} %fusion.85), channel_id=1, source_target_pairs={{0,8},{8,16},{16,24},{24,32},{32,40},{40,48},{48,56},{56,64},{64,7... | collective-permute-start | bytes 786440 | tf_op jit(solution)/shard_map/while/body/eval_jaxpr/ppermute | solution.py:17
  127.0 6.6 %collective-permute-done = bf16[2,1,8,64,128]{4,3,2,1,0:T(8,128)(2,1)S(1)} collective-permute-done((bf16[2,1,8,64,128]{4,3,2,1,0:T(8,128)(2,1)}, bf16[2,1,8,64,128]{4,3,2,1,0:T(8,128)(2,1)S(1)}, u32[]{:S(2)}, u32[]{:S(2)}) %collective-permute-start) | collective-permute-done | bytes 262176 | tf_op jit(solution)/shard_map/while/body/eval_jaxpr/ppermute | solution.py:17
  134.5 7.3 %collective-permute-start = (bf16[2,1,8,64,128]{4,3,2,1,0:T(8,128)(2,1)}, bf16[2,1,8,64,128]{4,3,2,1,0:T(8,128)(2,1)S(1)}, u32[]{:S(2)}, u32[]{:S(2)}) collective-permute-start(bf16[2,1,8,64,128]{4,3,2,1,0:T(8,128)(2,1)} %fusion.85), channel_id=1, source_target_pairs={{0,8},{8,16},{16,24},{24,32},{32,40},{40,48},{48,56},{56,64},{64,7... | collective-permute-start | bytes 786440 | tf_op jit(solution)/shard_map/while/body/eval_jaxpr/ppermute | solution.py:17
  141.8 6.3 %collective-permute-done = bf16[2,1,8,64,128]{4,3,2,1,0:T(8,128)(2,1)S(1)} collective-permute-done((bf16[2,1,8,64,128]{4,3,2,1,0:T(8,128)(2,1)}, bf16[2,1,8,64,128]{4,3,2,1,0:T(8,128)(2,1)S(1)}, u32[]{:S(2)}, u32[]{:S(2)}) %collective-permute-start) | collective-permute-done | bytes 262176 | tf_op jit(solution)/shard_map/while/body/eval_jaxpr/ppermute | solution.py:17
  148.9 6.3 %collective-permute-start = (bf16[2,1,8,64,128]{4,3,2,1,0:T(8,128)(2,1)}, bf16[2,1,8,64,128]{4,3,2,1,0:T(8,128)(2,1)S(1)}, u32[]{:S(2)}, u32[]{:S(2)}) collective-permute-start(bf16[2,1,8,64,128]{4,3,2,1,0:T(8,128)(2,1)} %fusion.85), channel_id=1, source_target_pairs={{0,8},{8,16},{16,24},{24,32},{32,40},{40,48},{48,56},{56,64},{64,7... | collective-permute-start | bytes 786440 | tf_op jit(solution)/shard_map/while/body/eval_jaxpr/ppermute | solution.py:17
  155.2 5.0 collective-permute-done
  161.2 5.6 collective-permute-start
  166.8 4.2 collective-permute-done
  171.9 6.4 %collective-permute-start = (bf16[2,1,8,64,128]{4,3,2,1,0:T(8,128)(2,1)}, bf16[2,1,8,64,128]{4,3,2,1,0:T(8,128)(2,1)S(1)}, u32[]{:S(2)}, u32[]{:S(2)}) collective-permute-start(bf16[2,1,8,64,128]{4,3,2,1,0:T(8,128)(2,1)} %fusion.85), channel_id=1, source_target_pairs={{0,8},{8,16},{16,24},{24,32},{32,40},{40,48},{48,56},{56,64},{64,7... | collective-permute-start | bytes 786440 | tf_op jit(solution)/shard_map/while/body/eval_jaxpr/ppermute | solution.py:17
  178.3 4.2 collective-permute-done
  183.3 6.4 %collective-permute-start = (bf16[2,1,8,64,128]{4,3,2,1,0:T(8,128)(2,1)}, bf16[2,1,8,64,128]{4,3,2,1,0:T(8,128)(2,1)S(1)}, u32[]{:S(2)}, u32[]{:S(2)}) collective-permute-start(bf16[2,1,8,64,128]{4,3,2,1,0:T(8,128)(2,1)} %fusion.85), channel_id=1, source_target_pairs={{0,8},{8,16},{16,24},{24,32},{32,40},{40,48},{48,56},{56,64},{64,7... | collective-permute-start | bytes 786440 | tf_op jit(solution)/shard_map/while/body/eval_jaxpr/ppermute | solution.py:17
  189.7 4.2 collective-permute-done
  196.1 4.2 fusion.20
  215.6 4.1 copy.130
  223.4 5.9 convolution_convert_fusion.2
  230.5 49.0 %reduce-scatter.3.cloned.1.call-done = bf16[128,2048]{1,0:T(8,128)(2,1)} async-done(((bf16[1024,2048]{1,0:T(8,128)(2,1)}), bf16[128,2048]{1,0:T(8,128)(2,1)}) %reduce-scatter.3.cloned.1.call-update) | async-done | bytes 524304 | tf_op jit(solution)/shard_map/reduce_scatter | solution.py:118
  283.1 7.8 %all_gather.6 = s32[1024,2]{0,1:T(2,128)S(1)} all-gather(s32[128,2]{0,1:T(2,128)S(1)} %reshape.403), channel_id=1, replica_groups=mesh['seq'=16,'exp'=8] {'exp'}, dimensions={0}, use_global_device_ids=true | all-gather | bytes 9216 | tf_op jit(solution)/shard_map/all_gather | solution.py:133
  291.8 4.6 reduce-window.16
  297.6 16.4 %all-gather.2.cloned.1.call-done = bf16[1024,2048]{1,0:T(8,128)(2,1)} async-done(((bf16[128,2048]{1,0:T(8,128)(2,1)}), bf16[1024,2048]{1,0:T(8,128)(2,1)}) %all-gather.2.cloned.1.call-update) | async-done | bytes 4194320 | tf_op jit(solution)/shard_map/all_gather | solution.py:132
  314.0 8.1 %convolution_convert_fusion.1 = bf16[8,272,2048]{2,1,0:T(8,128)(2,1)} fusion(pred[8,272,128]{2,1,0:T(8,128)(4,1)S(1)} %fusion.15, bf16[8,128,2048]{2,1,0:T(8,128)(2,1)} %bitcast.182), kind=kOutput, calls=%fused_computation.7 | convolution fusion | flops 1145307136 | bytes 13385728 | tf_op jit(solution)/shard_map/vmap()/dot_general | solution.py:30
  322.1 11.9 %copy.142 = bf16[8,272,2048]{2,0,1:T(8,128)(2,1)} copy(bf16[8,272,2048]{2,1,0:T(8,128)(2,1)} %convolution_convert_fusion.1) | data formatting | bytes 17825792 | tf_op jit(solution)/shard_map/vmap()/convert_element_type | solution.py:30
  334.0 108.9 %all_to_all.10 = bf16[8,16,17,2048]{3,0,2,1:T(8,128)(2,1)S(1)} all-to-all(bf16[8,16,17,2048]{3,0,2,1:T(8,128)(2,1)} %bitcast.180), channel_id=1, replica_groups=mesh['seq'=16,'exp'=8] {'seq'}, dimensions={1} | all-to-all | bytes 17825792 | tf_op jit(solution)/shard_map/all_to_all | solution.py:142
  442.9 16.4 %copy.143 = bf16[8,16,17,2048]{3,2,1,0:T(8,128)(2,1)} copy(bf16[8,16,17,2048]{3,0,2,1:T(8,128)(2,1)S(1)} %all_to_all.10) | data formatting | bytes 17825792 | tf_op jit(solution)/shard_map/all_to_all | solution.py:142
  459.4 14.2 %reshape.407 = bf16[2176,2048]{1,0:T(8,128)(2,1)} reshape(bf16[8,16,17,2048]{3,2,1,0:T(8,128)(2,1)} %copy.143) | data formatting | bytes 17825792 | tf_op jit(solution)/shard_map/reshape | solution.py:149
  473.6 14.9 %fusion.13 = f32[2176,896]{1,0:T(8,128)} fusion(bf16[2176,2048]{1,0:T(8,128)(2,1)} %reshape.407, bf16[1,2048,896]{2,1,0:T(8,128)(2,1)} %param.30), kind=kOutput, calls=%fused_computation.19 | convolution fusion | flops 7985954816 | bytes 20381696 | tf_op jit(solution)/shard_map/dot_general | solution.py:150
  488.5 25.5 %convolution_convert_fusion = bf16[2176,2048]{1,0:T(8,128)(2,1)} fusion(f32[2176,896]{1,0:T(8,128)} %fusion.13, bf16[2176,2048]{1,0:T(8,128)(2,1)} %reshape.407, bf16[1,896,2048]{2,1,0:T(8,128)(2,1)} %param.32, bf16[1,2048,896]{2,1,0:T(8,128)(2,1)} %param.31), kind=kOutput, calls=%fused_computation.4 | convolution fusion | flops 15988064256 | bytes 32964608 | tf_op jit(solution)/shard_map/dot_general | solution.py:157
  514.7 50.8 %reduce-scatter.5.cloned.1.call-done = bf16[272,2048]{1,0:T(8,128)(2,1)} async-done(((bf16[2176,2048]{1,0:T(8,128)(2,1)}), bf16[272,2048]{1,0:T(8,128)(2,1)}) %reduce-scatter.5.cloned.1.call-update) | async-done | bytes 1114128 | tf_op jit(solution)/shard_map/reduce_scatter | solution.py:156
  568.0 7.3 %all-to-all-start.1 = ((bf16[16,17,2048]{2,1,0:T(8,128)(2,1)}), bf16[16,17,2048]{2,1,0:T(8,128)(2,1)}, u32[]{:S(2)}, u32[]{:S(2)}) async-start(bf16[16,17,2048]{2,1,0:T(8,128)(2,1)} %reshape.408), calls=%async_computation.3 | async-start | bytes 3145728 | tf_op jit(solution)/shard_map/all_to_all | solution.py:162
  581.7 16.7 %all-to-all-done.1 = bf16[16,17,2048]{2,1,0:T(8,128)(2,1)} async-done(((bf16[16,17,2048]{2,1,0:T(8,128)(2,1)}), bf16[16,17,2048]{2,1,0:T(8,128)(2,1)}, u32[]{:S(2)}, u32[]{:S(2)}) %all-to-all-start.1) | async-done | bytes 1114144 | tf_op jit(solution)/shard_map/all_to_all | solution.py:162
  604.1 4.1 multiply_reduce_fusion
  (138 shorter events, 82.0 us)
Async XLA Ops:
  6.5 216.9 %copy-start = (bf16[512,2048]{1,0:T(8,128)(2,1)S(1)}, bf16[512,2048]{1,0:T(8,128)(2,1)}, u32[]{:S(2)}) copy-start(bf16[512,2048]{1,0:T(8,128)(2,1)} %param.27) | copy-start | bytes 6291460
  6.5 13.5 %copy-start.3 = (bf16[512,2,128]{2,1,0:T(2,128)(2,1)S(1)}, bf16[512,2,128]{2,1,0:T(2,128)(2,1)}, u32[]{:S(2)}) copy-start(bf16[512,2,128]{2,1,0:T(2,128)(2,1)} %param.21) | copy-start | bytes 786436
  6.5 272.9 %reduce-scatter.3.cloned.1.call-start = ((), (), s32[]{:S(2)}) async-start(), calls=%async_computation.4 | async-start | bytes 4718592 | tf_op jit(solution)/shard_map/reduce_scatter | solution.py:118
  24.6 9.8 %collective-permute-start = (bf16[2,1,8,64,128]{4,3,2,1,0:T(8,128)(2,1)}, bf16[2,1,8,64,128]{4,3,2,1,0:T(8,128)(2,1)S(1)}, u32[]{:S(2)}, u32[]{:S(2)}) collective-permute-start(bf16[2,1,8,64,128]{4,3,2,1,0:T(8,128)(2,1)} %fusion.85), channel_id=1, source_target_pairs={{0,8},{8,16},{16,24},{24,32},{32,40},{40,48},{48,56},{56,64},{64,7... | collective-permute-start | bytes 786440 | tf_op jit(solution)/shard_map/while/body/eval_jaxpr/ppermute | solution.py:17
  35.3 9.3 %collective-permute-start = (bf16[2,1,8,64,128]{4,3,2,1,0:T(8,128)(2,1)}, bf16[2,1,8,64,128]{4,3,2,1,0:T(8,128)(2,1)S(1)}, u32[]{:S(2)}, u32[]{:S(2)}) collective-permute-start(bf16[2,1,8,64,128]{4,3,2,1,0:T(8,128)(2,1)} %fusion.85), channel_id=1, source_target_pairs={{0,8},{8,16},{16,24},{24,32},{32,40},{40,48},{48,56},{56,64},{64,7... | collective-permute-start | bytes 786440 | tf_op jit(solution)/shard_map/while/body/eval_jaxpr/ppermute | solution.py:17
  45.4 8.5 %collective-permute-start = (bf16[2,1,8,64,128]{4,3,2,1,0:T(8,128)(2,1)}, bf16[2,1,8,64,128]{4,3,2,1,0:T(8,128)(2,1)S(1)}, u32[]{:S(2)}, u32[]{:S(2)}) collective-permute-start(bf16[2,1,8,64,128]{4,3,2,1,0:T(8,128)(2,1)} %fusion.85), channel_id=1, source_target_pairs={{0,8},{8,16},{16,24},{24,32},{32,40},{40,48},{48,56},{56,64},{64,7... | collective-permute-start | bytes 786440 | tf_op jit(solution)/shard_map/while/body/eval_jaxpr/ppermute | solution.py:17
  54.8 8.5 %collective-permute-start = (bf16[2,1,8,64,128]{4,3,2,1,0:T(8,128)(2,1)}, bf16[2,1,8,64,128]{4,3,2,1,0:T(8,128)(2,1)S(1)}, u32[]{:S(2)}, u32[]{:S(2)}) collective-permute-start(bf16[2,1,8,64,128]{4,3,2,1,0:T(8,128)(2,1)} %fusion.85), channel_id=1, source_target_pairs={{0,8},{8,16},{16,24},{24,32},{32,40},{40,48},{48,56},{56,64},{64,7... | collective-permute-start | bytes 786440 | tf_op jit(solution)/shard_map/while/body/eval_jaxpr/ppermute | solution.py:17
  64.1 8.5 %collective-permute-start = (bf16[2,1,8,64,128]{4,3,2,1,0:T(8,128)(2,1)}, bf16[2,1,8,64,128]{4,3,2,1,0:T(8,128)(2,1)S(1)}, u32[]{:S(2)}, u32[]{:S(2)}) collective-permute-start(bf16[2,1,8,64,128]{4,3,2,1,0:T(8,128)(2,1)} %fusion.85), channel_id=1, source_target_pairs={{0,8},{8,16},{16,24},{24,32},{32,40},{40,48},{48,56},{56,64},{64,7... | collective-permute-start | bytes 786440 | tf_op jit(solution)/shard_map/while/body/eval_jaxpr/ppermute | solution.py:17
  73.5 9.6 %collective-permute-start = (bf16[2,1,8,64,128]{4,3,2,1,0:T(8,128)(2,1)}, bf16[2,1,8,64,128]{4,3,2,1,0:T(8,128)(2,1)S(1)}, u32[]{:S(2)}, u32[]{:S(2)}) collective-permute-start(bf16[2,1,8,64,128]{4,3,2,1,0:T(8,128)(2,1)} %fusion.85), channel_id=1, source_target_pairs={{0,8},{8,16},{16,24},{24,32},{32,40},{40,48},{48,56},{56,64},{64,7... | collective-permute-start | bytes 786440 | tf_op jit(solution)/shard_map/while/body/eval_jaxpr/ppermute | solution.py:17
  84.0 10.6 %collective-permute-start = (bf16[2,1,8,64,128]{4,3,2,1,0:T(8,128)(2,1)}, bf16[2,1,8,64,128]{4,3,2,1,0:T(8,128)(2,1)S(1)}, u32[]{:S(2)}, u32[]{:S(2)}) collective-permute-start(bf16[2,1,8,64,128]{4,3,2,1,0:T(8,128)(2,1)} %fusion.85), channel_id=1, source_target_pairs={{0,8},{8,16},{16,24},{24,32},{32,40},{40,48},{48,56},{56,64},{64,7... | collective-permute-start | bytes 786440 | tf_op jit(solution)/shard_map/while/body/eval_jaxpr/ppermute | solution.py:17
  95.5 10.7 %collective-permute-start = (bf16[2,1,8,64,128]{4,3,2,1,0:T(8,128)(2,1)}, bf16[2,1,8,64,128]{4,3,2,1,0:T(8,128)(2,1)S(1)}, u32[]{:S(2)}, u32[]{:S(2)}) collective-permute-start(bf16[2,1,8,64,128]{4,3,2,1,0:T(8,128)(2,1)} %fusion.85), channel_id=1, source_target_pairs={{0,8},{8,16},{16,24},{24,32},{32,40},{40,48},{48,56},{56,64},{64,7... | collective-permute-start | bytes 786440 | tf_op jit(solution)/shard_map/while/body/eval_jaxpr/ppermute | solution.py:17
  107.0 12.0 %collective-permute-start = (bf16[2,1,8,64,128]{4,3,2,1,0:T(8,128)(2,1)}, bf16[2,1,8,64,128]{4,3,2,1,0:T(8,128)(2,1)S(1)}, u32[]{:S(2)}, u32[]{:S(2)}) collective-permute-start(bf16[2,1,8,64,128]{4,3,2,1,0:T(8,128)(2,1)} %fusion.85), channel_id=1, source_target_pairs={{0,8},{8,16},{16,24},{24,32},{32,40},{40,48},{48,56},{56,64},{64,7... | collective-permute-start | bytes 786440 | tf_op jit(solution)/shard_map/while/body/eval_jaxpr/ppermute | solution.py:17
  120.0 13.6 %collective-permute-start = (bf16[2,1,8,64,128]{4,3,2,1,0:T(8,128)(2,1)}, bf16[2,1,8,64,128]{4,3,2,1,0:T(8,128)(2,1)S(1)}, u32[]{:S(2)}, u32[]{:S(2)}) collective-permute-start(bf16[2,1,8,64,128]{4,3,2,1,0:T(8,128)(2,1)} %fusion.85), channel_id=1, source_target_pairs={{0,8},{8,16},{16,24},{24,32},{32,40},{40,48},{48,56},{56,64},{64,7... | collective-permute-start | bytes 786440 | tf_op jit(solution)/shard_map/while/body/eval_jaxpr/ppermute | solution.py:17
  134.5 13.6 %collective-permute-start = (bf16[2,1,8,64,128]{4,3,2,1,0:T(8,128)(2,1)}, bf16[2,1,8,64,128]{4,3,2,1,0:T(8,128)(2,1)S(1)}, u32[]{:S(2)}, u32[]{:S(2)}) collective-permute-start(bf16[2,1,8,64,128]{4,3,2,1,0:T(8,128)(2,1)} %fusion.85), channel_id=1, source_target_pairs={{0,8},{8,16},{16,24},{24,32},{32,40},{40,48},{48,56},{56,64},{64,7... | collective-permute-start | bytes 786440 | tf_op jit(solution)/shard_map/while/body/eval_jaxpr/ppermute | solution.py:17
  148.9 11.4 %collective-permute-start = (bf16[2,1,8,64,128]{4,3,2,1,0:T(8,128)(2,1)}, bf16[2,1,8,64,128]{4,3,2,1,0:T(8,128)(2,1)S(1)}, u32[]{:S(2)}, u32[]{:S(2)}) collective-permute-start(bf16[2,1,8,64,128]{4,3,2,1,0:T(8,128)(2,1)} %fusion.85), channel_id=1, source_target_pairs={{0,8},{8,16},{16,24},{24,32},{32,40},{40,48},{48,56},{56,64},{64,7... | collective-permute-start | bytes 786440 | tf_op jit(solution)/shard_map/while/body/eval_jaxpr/ppermute | solution.py:17
  161.2 9.8 %collective-permute-start = (bf16[2,1,8,64,128]{4,3,2,1,0:T(8,128)(2,1)}, bf16[2,1,8,64,128]{4,3,2,1,0:T(8,128)(2,1)S(1)}, u32[]{:S(2)}, u32[]{:S(2)}) collective-permute-start(bf16[2,1,8,64,128]{4,3,2,1,0:T(8,128)(2,1)} %fusion.85), channel_id=1, source_target_pairs={{0,8},{8,16},{16,24},{24,32},{32,40},{40,48},{48,56},{56,64},{64,7... | collective-permute-start | bytes 786440 | tf_op jit(solution)/shard_map/while/body/eval_jaxpr/ppermute | solution.py:17
  171.9 10.6 %collective-permute-start = (bf16[2,1,8,64,128]{4,3,2,1,0:T(8,128)(2,1)}, bf16[2,1,8,64,128]{4,3,2,1,0:T(8,128)(2,1)S(1)}, u32[]{:S(2)}, u32[]{:S(2)}) collective-permute-start(bf16[2,1,8,64,128]{4,3,2,1,0:T(8,128)(2,1)} %fusion.85), channel_id=1, source_target_pairs={{0,8},{8,16},{16,24},{24,32},{32,40},{40,48},{48,56},{56,64},{64,7... | collective-permute-start | bytes 786440 | tf_op jit(solution)/shard_map/while/body/eval_jaxpr/ppermute | solution.py:17
  183.3 10.6 %collective-permute-start = (bf16[2,1,8,64,128]{4,3,2,1,0:T(8,128)(2,1)}, bf16[2,1,8,64,128]{4,3,2,1,0:T(8,128)(2,1)S(1)}, u32[]{:S(2)}, u32[]{:S(2)}) collective-permute-start(bf16[2,1,8,64,128]{4,3,2,1,0:T(8,128)(2,1)} %fusion.85), channel_id=1, source_target_pairs={{0,8},{8,16},{16,24},{24,32},{32,40},{40,48},{48,56},{56,64},{64,7... | collective-permute-start | bytes 786440 | tf_op jit(solution)/shard_map/while/body/eval_jaxpr/ppermute | solution.py:17
  203.3 7.7 %copy-start.9 = (f32[8]{0:T(128)S(1)}, f32[8]{0:T(128)}, u32[]{:S(2)}) copy-start(f32[8]{0:T(128)} %param.25) | copy-start | bytes 100
  203.3 7.8 %copy-start.2 = (bf16[512,2,512]{0,2,1:T(8,128)(2,1)S(1)}, bf16[512,2,512]{0,2,1:T(8,128)(2,1)}, u32[]{:S(2)}) copy-start(bf16[512,2,512]{0,2,1:T(8,128)(2,1)} %copy.120) | copy-start | bytes 3145732
  215.6 7.8 %copy-start.10 = (f32[512]{0:T(512)S(1)}, f32[512]{0:T(512)}, u32[]{:S(2)}) copy-start(f32[512]{0:T(512)} %param.26) | copy-start | bytes 6148
  229.3 1.0 copy-start.4
  229.3 51.5 %copy-start.6 = (f32[2048]{0:T(1024)S(1)}, f32[2048]{0:T(1024)}, u32[]{:S(2)}) copy-start(f32[2048]{0:T(1024)} %param.29) | copy-start | bytes 24580
  229.3 53.5 %copy-start.7 = (s32[64,2,2]{0,2,1:T(2,128)S(1)}, s32[64,2,2]{0,2,1:T(2,128)}, u32[]{:S(2)}) copy-start(s32[64,2,2]{0,2,1:T(2,128)} %param.33) | copy-start | bytes 3076
  229.3 84.6 %all-gather.2.cloned.1.call-start = ((), (), s32[]{:S(2)}) async-start(), calls=%async_computation.5 | async-start | bytes 4718592 | tf_op jit(solution)/shard_map/all_gather | solution.py:132
  282.8 282.7 %reduce-scatter.5.cloned.1.call-start = ((), (), s32[]{:S(2)}) async-start(), calls=%async_computation.6 | async-start | bytes 10027008 | tf_op jit(solution)/shard_map/reduce_scatter | solution.py:156
  513.9 0.8 copy-start.5
  514.0 62.6 %copy-start.8 = (f32[64,2,2]{0,2,1:T(2,128)S(1)}, f32[64,2,2]{0,2,1:T(2,128)}, u32[]{:S(2)}) copy-start(f32[64,2,2]{0,2,1:T(2,128)} %param.34) | copy-start | bytes 3076
  568.0 30.5 %all-to-all-start.1 = ((bf16[16,17,2048]{2,1,0:T(8,128)(2,1)}), bf16[16,17,2048]{2,1,0:T(8,128)(2,1)}, u32[]{:S(2)}, u32[]{:S(2)}) async-start(bf16[16,17,2048]{2,1,0:T(8,128)(2,1)} %reshape.408), calls=%async_computation.3 | async-start | bytes 3145728 | tf_op jit(solution)/shard_map/all_to_all | solution.py:162
  608.2 7.3 %copy-start.1 = (bf16[512,2048]{1,0:T(8,128)(2,1)S(1)}, bf16[512,2048]{1,0:T(8,128)(2,1)}, u32[]{:S(2)}) copy-start(bf16[512,2048]{1,0:T(8,128)(2,1)} %param.27) | copy-start | bytes 6291460
Sparse Core Ops, SparseCore 0:
  229.4 49.9 reduce-scatter.2
  282.9 31.0 all-gather.1
  514.1 51.3 reduce-scatter.4
where the time goes:
time: 633 us; the launch traced here: 623 us
  waiting for transfers between devices  205 us (32%)
  blocking collectives  117 us (18%)
  starting transfers between devices  92.5 us (15%)
  local copies, waits for them, and re-layouts  82.5 us (13%)
  matrix products  67.6 us (11%)
  other arithmetic  41.6 us (7%)
  between operations  16.5 us (3%)
    all_to_all x1, blocking collectives, on_device(): lax.all_to_all(buffers.reshape(columns, experts, capacity, D), 'seq', spl...  109 us
    ppermute x15, starting transfers between devices, shifted(): return lax.ppermute(block, axis, route)  85 us
    ppermute x15, waiting for transfers between devices, shifted(): return lax.ppermute(block, axis, route)  71.7 us
    reduce_scatter x1, waiting for transfers between devices, on_device(): lax.psum_scatter(jnp.dot(piece, w_down[0], preferred_element_type=jnp.flo...  50.8 us
    reduce_scatter x1, waiting for transfers between devices, on_device(): lax.psum_scatter(jnp.dot(piece, w_out, preferred_element_type=jnp.float32...  49 us
    dot_general x1, matrix products, on_device(): jnp.dot(piece, w_down[0], preferred_element_type=jnp.float32)  25.5 us
    all_to_all x1, waiting for transfers between devices, on_device(): lax.all_to_all(summed.reshape(experts, capacity, D), 'seq', split_axis=0,...  16.7 us
    all_to_all x1, local copies, waits for them, and re-layouts, on_device(): lax.all_to_all(buffers.reshape(columns, experts, capacity, D), 'seq', spl...  16.4 us
  transfers between devices with their start and end apart: 19, of which 19 were waited for; matrix products, arithmetic and copies ran while one was open for 2% of the time, Pallas kernels for 0%

commit v1 on v0

--- a/solution.py
+++ b/solution.py
@@ -9,26 +9,6 @@
 STATE = 128
 GROUPS = 8
 BLOCK = 256
-
-
-def shifted(block, axis, distance):
-    devices = range(lax.axis_size(axis))
-    route = [(i - distance, i) for i in devices if i - distance in devices]
-    return lax.ppermute(block, axis, route)
-
-
-def build_slots(tokens, chosen, experts, capacity):
-    picks = chosen.reshape(-1)
-    onehot = (picks[:, None] == jnp.arange(experts, dtype=jnp.int32)[None, :]).astype(jnp.int32)
-    before = jnp.cumsum(onehot, axis=0) - onehot
-    ranked = jnp.sum(before * onehot, axis=1)
-    places = picks * capacity + ranked
-    layout = jnp.arange(experts * capacity, dtype=jnp.int32)
-    select = jnp.any(layout[:, None, None] == places.reshape(-1, 2)[None, :, :], axis=2).astype(
-        jnp.bfloat16
-    )
-    buffer = jnp.dot(select, tokens, preferred_element_type=jnp.float32).astype(jnp.bfloat16)
-    return (buffer, places)
 
 
 def on_device(
@@ -91,12 +71,32 @@
         running = through[index][..., None, None] * running + contrib[index]
         carried = carried * through[index]
 
-    def link(turn, state):
-        return shifted(
-            (carried[..., None, None] * state + running).astype(jnp.bfloat16), "seq", 1
-        ).astype(jnp.float32)
-
-    entering = lax.fori_loop(0, lax.axis_size("seq") - 1, link, jnp.zeros_like(running))
+    ranks = lax.axis_size("seq")
+    flat_carried = carried.reshape(ranks, 1, 1)
+    high = lax.reduce_precision(flat_carried, 8, 7)
+    middle = lax.reduce_precision(flat_carried - high, 8, 7)
+    low = flat_carried - high - middle
+    row = lax.broadcasted_iota(jnp.int32, (ranks, 8, STATE), 1)
+    extra = jnp.where(row == 0, high, jnp.where(row == 1, middle, jnp.where(row == 2, low, 0.0)))
+    parcel = jnp.concatenate(
+        [running.reshape(ranks, HEAD_DIM, STATE), extra], axis=1
+    ).astype(jnp.bfloat16)
+    parcels = lax.all_to_all(parcel, "seq", split_axis=0, concat_axis=0, tiled=True).astype(
+        jnp.float32
+    )
+    state = jnp.zeros((HEAD_DIM, STATE), jnp.float32)
+    states = [state]
+    for rank in range(ranks - 1):
+        factor = parcels[rank, HEAD_DIM] + parcels[rank, HEAD_DIM + 1] + parcels[rank, HEAD_DIM + 2]
+        state = factor[None, :] * state + parcels[rank, :HEAD_DIM]
+        states.append(state)
+    entering = (
+        lax.all_to_all(
+            jnp.stack(states).astype(jnp.bfloat16), "seq", split_axis=0, concat_axis=0, tiled=True
+        )
+        .astype(jnp.float32)
+        .reshape(running.shape)
+    )
     begin = jnp.stack(starts) + jnp.stack(prefixes)[..., None, None] * entering[None]
     readout = jnp.einsum(
         "cbgipn,ctbgn->ctbgip", begin, reads.astype(jnp.float32), precision=lax.Precision.HIGHEST
@@ -127,41 +127,41 @@
     experts = lax.axis_size("seq")
     capacity = max(2, 2 * rows_keep * 17 // (16 * experts))
     chosen = routes.reshape(rows_keep, 2)
-    hidden_units = w_gate.shape[2]
-    all_tokens, all_routes = (
-        lax.all_gather(moe_in, "exp", axis=0, tiled=True),
-        lax.all_gather(chosen, "exp", axis=0, tiled=True),
-    )
-    buffers, all_places = jax.vmap(build_slots, in_axes=(0, 0, None, None))(
-        all_tokens.reshape(columns, rows_keep, D),
-        all_routes.reshape(columns, rows_keep, 2),
-        experts,
-        capacity,
-    )
-    places = lax.dynamic_index_in_dim(all_places, lax.axis_index("exp"), 0, keepdims=False)
-    arrived = lax.all_to_all(
-        buffers.reshape(columns, experts, capacity, D),
-        "seq",
-        split_axis=1,
-        concat_axis=1,
-        tiled=True,
-    )
-    rows = arrived.reshape(-1, D)
-    gate_value = jnp.dot(rows, w_gate[0], preferred_element_type=jnp.float32)
-    up_value = jnp.dot(rows, w_up[0], preferred_element_type=jnp.float32)
-    hidden = (jax.nn.silu(gate_value) * up_value).astype(jnp.bfloat16)
-    hidden_all = hidden.reshape(arrived.shape[:-1] + (hidden_units,))
-    flat_hidden = hidden_all.reshape(-1, hidden_units)
-    piece = flat_hidden
-    summed = lax.psum_scatter(
-        jnp.dot(piece, w_down[0], preferred_element_type=jnp.float32).astype(jnp.bfloat16),
-        "exp",
-        scatter_dimension=0,
-        tiled=True,
-    )
-    returned = lax.all_to_all(
-        summed.reshape(experts, capacity, D), "seq", split_axis=0, concat_axis=0, tiled=True
-    )
+    picks = chosen.reshape(-1)
+    onehot = (picks[:, None] == jnp.arange(experts, dtype=jnp.int32)[None, :]).astype(jnp.int32)
+    before = jnp.cumsum(onehot, axis=0) - onehot
+    ranked = jnp.sum(before * onehot, axis=1)
+    places = picks * capacity + ranked
+    pairs = places.reshape(-1, 2)
+    first = (capacity + 1) // 2
+    returned = []
+    for start, count in ((0, first), (first, capacity - first)):
+        layout = (
+            jnp.arange(experts, dtype=jnp.int32)[:, None] * capacity
+            + start
+            + jnp.arange(count, dtype=jnp.int32)[None, :]
+        ).reshape(-1)
+        select = jnp.any(layout[:, None, None] == pairs[None, :, :], axis=2).astype(jnp.bfloat16)
+        slots = jnp.dot(select, moe_in, preferred_element_type=jnp.float32).astype(jnp.bfloat16)
+        arrived = lax.all_to_all(
+            slots.reshape(experts, count, D), "seq", split_axis=0, concat_axis=0, tiled=True
+        )
+        rows = lax.all_gather(arrived.reshape(experts * count, D), "exp", axis=0, tiled=True)
+        gate_value = jnp.dot(rows, w_gate[0], preferred_element_type=jnp.float32)
+        up_value = jnp.dot(rows, w_up[0], preferred_element_type=jnp.float32)
+        hidden = (jax.nn.silu(gate_value) * up_value).astype(jnp.bfloat16)
+        summed = lax.psum_scatter(
+            jnp.dot(hidden, w_down[0], preferred_element_type=jnp.float32).astype(jnp.bfloat16),
+            "exp",
+            scatter_dimension=0,
+            tiled=True,
+        )
+        returned.append(
+            lax.all_to_all(
+                summed.reshape(experts, count, D), "seq", split_axis=0, concat_axis=0, tiled=True
+            )
+        )
+    returned = jnp.concatenate(returned, axis=1)
     picked = (
         jnp.take(returned.reshape(experts * capacity, D), places, axis=0)
         .astype(jnp.float32)

time: 633 us -> 347 us (0.55)
  blocking collectives: 117 us -> 33.1 us
  waiting for transfers between devices: 205 us -> 130 us
  starting transfers between devices: 92.5 us -> 29.1 us
  local copies, waits for them, and re-layouts: 82.5 us -> 39.2 us
  matrix products: 67.6 us -> 57 us
    ppermute x15 -> x0, starting transfers between devices: 85 us -> none  [shifted(): return lax.ppermute(block, axis, route)]
    all_to_all x1 -> x2, blocking collectives: 109 us -> 33.1 us  [on_device(): lax.all_to_all(slots.reshape(experts, count, D), 'seq', split_axis=0, con...]
    ppermute x15 -> x0, waiting for transfers between devices: 71.7 us -> none  [shifted(): return lax.ppermute(block, axis, route)]
    all_to_all x1 -> x4, starting transfers between devices: 7.25 us -> 28 us  [the longest x2 14.2 us: on_device(): lax.all_to_all(summed.reshape(experts, count, D), 'seq', split_axis=0, co...]
    all_to_all x1 -> x0, local copies, waits for them, and re-layouts: 16.4 us -> none  [on_device(): lax.all_to_all(buffers.reshape(columns, experts, capacity, D), 'seq', spl...]
    reduce_scatter x1, waiting for transfers between devices: 49 us -> 33.2 us  [on_device(): lax.psum_scatter(jnp.dot(piece, w_out, preferred_element_type=jnp.float32...]
    reshape x3, local copies, waits for them, and re-layouts: 16.8 us -> 3.66 us  [the longest x1 2.29 us: on_device(): summed.reshape(experts, count, D)]
    convert_element_type x31 -> x2, other arithmetic: 13 us -> 0.05 us  [the longest x1 0.04 us: on_device(): lax.all_to_all(parcel, 'seq', split_axis=0, concat_axis=0, tiled=True)]
  transfers between devices with their start and end apart: 19 -> 9, of which waited for: 19 -> 8; matrix products, arithmetic and copies ran while one was open for 2% -> 17% of each run, Pallas kernels for 0% -> 0%
where the time goes in v1:
time: 347 us; the launch traced here: 341 us
  waiting for transfers between devices  130 us (37%)
  matrix products  57 us (16%)
  local copies, waits for them, and re-layouts  39.2 us (11%)
  other arithmetic  36.2 us (10%)
  blocking collectives  33.1 us (10%)
  starting transfers between devices  29.1 us (8%)
  between operations  16.6 us (5%)
    reduce_scatter x2, waiting for transfers between devices, on_device(): lax.psum_scatter(jnp.dot(hidden, w_down[0], preferred_element_type=jnp.fl...  49.9 us
    reduce_scatter x1, waiting for transfers between devices, on_device(): lax.psum_scatter(jnp.dot(piece, w_out, preferred_element_type=jnp.float32...  33.2 us
    all_to_all x2, blocking collectives, on_device(): lax.all_to_all(slots.reshape(experts, count, D), 'seq', split_axis=0, con...  33.1 us
    all_gather x2, waiting for transfers between devices, on_device(): lax.all_gather(arrived.reshape(experts * count, D), 'exp', axis=0, tiled=...  27.7 us
    all_to_all x2, starting transfers between devices, on_device(): lax.all_to_all(summed.reshape(experts, count, D), 'seq', split_axis=0, co...  14.2 us
    dot_general x2, matrix products, on_device(): gate_value = jnp.dot(rows, w_gate[0], preferred_element_type=jnp.float32)  12.9 us
    dot_general x2, matrix products, on_device(): jnp.dot(hidden, w_down[0], preferred_element_type=jnp.float32)  12.8 us
    dot_general x2, matrix products, on_device(): up_value = jnp.dot(rows, w_up[0], preferred_element_type=jnp.float32)  12.8 us
  transfers between devices with their start and end apart: 9, of which 8 were waited for; matrix products, arithmetic and copies ran while one was open for 17% of the time, Pallas kernels for 0%

profile of v1, /device:TPU:0, one launch (start us, length us, event | category | flops | bytes accessed | tf_op | source)
XLA Modules:
  0.0 341.1 jit_solution(10356479938638588427)
XLA Ops:
  7.5 2.3 reduce-window.14
  11.0 2.4 copy.83
  13.4 1.1 reshape.1400
  15.5 2.3 multiply_convert_fusion.4
  20.4 8.0 %all-to-all-start = ((bf16[16,72,128]{2,1,0:T(8,128)(2,1)}), bf16[16,72,128]{2,1,0:T(8,128)(2,1)S(1)}, u32[]{:S(2)}, u32[]{:S(2)}) async-start(bf16[16,72,128]{2,1,0:T(8,128)(2,1)} %pad_maximum_fusion.1), calls=%async_computation | async-start | bytes 589824 | tf_op jit(solution)/shard_map/all_to_all | solution.py:84
  29.6 3.7 %copy.91 = bf16[512,2,512]{0,2,1:T(8,128)(2,1)} copy(bf16[512,2,512]{2,1,0:T(2,128)(2,1)} %param.18) | data formatting | bytes 2097152 | tf_op args[1]
  33.4 2.4 fusion.59
  35.8 1.4 all-to-all-done
  46.4 5.8 %all-to-all-start.1 = ((bf16[16,64,128]{2,1,0:T(8,128)(2,1)}), bf16[16,64,128]{2,1,0:T(8,128)(2,1)S(1)}, u32[]{:S(2)}, u32[]{:S(2)}) async-start(bf16[16,64,128]{2,1,0:T(8,128)(2,1)} %constant_dynamic-update-slice_fusion), calls=%async_computation.1 | async-start | bytes 524288 | tf_op jit(solution)/shard_map/all_to_all | solution.py:94
  52.8 1.9 bitcast_add_fusion.2
  54.7 6.0 %all-to-all-done.1 = bf16[16,64,128]{2,1,0:T(8,128)(2,1)S(1)} async-done(((bf16[16,64,128]{2,1,0:T(8,128)(2,1)}), bf16[16,64,128]{2,1,0:T(8,128)(2,1)S(1)}, u32[]{:S(2)}, u32[]{:S(2)}) %all-to-all-start.1) | async-done | bytes 262176 | tf_op jit(solution)/shard_map/all_to_all | solution.py:94
  60.8 2.3 fusion.31
  63.2 2.8 fusion.26
  65.9 2.9 copy.89
  68.9 3.9 %reshape.1404 = f32[512,2,512]{0,2,1:T(8,128)} reshape(f32[2,256,2,1,8,64]{1,0,5,4,2,3:T(2,128)} %copy.89) | data formatting | bytes 4194304 | tf_op jit(solution)/shard_map/reshape | solution.py:105
  72.8 2.9 multiply_reduce_fusion.1
  75.7 1.5 broadcast_multiply_fusion
  77.2 4.1 %copy.92 = f32[512,2,512]{2,1,0:T(2,128)} copy(f32[512,2,512]{0,2,1:T(8,128)} %broadcast_multiply_fusion) | data formatting | bytes 4194304 | tf_op jit(solution)/shard_map/mul | solution.py:111
  81.4 3.7 %reshape.1405 = f32[1024,512]{1,0:T(8,128)} reshape(f32[512,2,512]{2,1,0:T(2,128)} %copy.92) | data formatting | bytes 4194304 | tf_op jit(solution)/shard_map/reshape | solution.py:111
  85.1 5.9 %convolution_convert_fusion.1 = bf16[1024,2048]{1,0:T(8,128)(2,1)} fusion(bf16[512,2048]{1,0:T(8,128)(2,1)S(1)} %copy-done, f32[1024,512]{1,0:T(8,128)} %reshape.1405, f32[512]{0:T(512)S(1)} %copy-done.22), kind=kOutput, calls=%fused_computation.11 | convolution fusion | flops 2150629376 | bytes 8390656 | tf_op jit(solution)/shard_map/dot_general | solution.py:119
  93.9 33.2 %reduce-scatter.4.cloned.1.call-done = bf16[128,2048]{1,0:T(8,128)(2,1)} async-done(((bf16[1024,2048]{1,0:T(8,128)(2,1)}), bf16[128,2048]{1,0:T(8,128)(2,1)}) %reduce-scatter.4.cloned.1.call-update) | async-done | bytes 524304 | tf_op jit(solution)/shard_map/reduce_scatter | solution.py:118
  127.1 1.3 multiply_reduce_fusion.2
  128.4 1.2 multiply_convert_fusion.8
  129.9 16.9 %all_to_all.30 = bf16[16,8,2048]{2,1,0:T(8,128)(2,1)} all-to-all(bf16[16,8,2048]{2,1,0:T(8,128)(2,1)S(1)} %fusion.21), channel_id=1, replica_groups=mesh['seq'=16,'exp'=8] {'seq'}, dimensions={0} | all-to-all | bytes 1048576 | tf_op jit(solution)/shard_map/all_to_all | solution.py:146
  147.7 16.2 %all_to_all.31 = bf16[16,9,2048]{2,1,0:T(8,128)(2,1)S(1)} all-to-all(bf16[16,9,2048]{2,1,0:T(8,128)(2,1)S(1)} %reshape.1407), channel_id=1, replica_groups=mesh['seq'=16,'exp'=8] {'seq'}, dimensions={0} | all-to-all | bytes 1179648 | tf_op jit(solution)/shard_map/all_to_all | solution.py:146
  163.9 1.1 reshape.1408
  165.1 10.4 %all-gather.5.cloned.1.call-done = bf16[1024,2048]{1,0:T(8,128)(2,1)} async-done(((bf16[128,2048]{1,0:T(8,128)(2,1)}), bf16[1024,2048]{1,0:T(8,128)(2,1)}) %all-gather.5.cloned.1.call-update) | async-done | bytes 4194320 | tf_op jit(solution)/shard_map/all_gather | solution.py:149
  175.5 7.5 %fusion.9 = f32[1024,896]{1,0:T(8,128)S(1)} fusion(bf16[1024,2048]{1,0:T(8,128)(2,1)} %all-gather.5.cloned.1.call-done, bf16[1,2048,896]{2,1,0:T(8,128)(2,1)} %param.29), kind=kOutput, calls=%fused_computation.15 | convolution fusion | flops 3758096384 | bytes 11534336 | tf_op jit(solution)/shard_map/dot_general | solution.py:151
  183.1 4.7 %multiply_convert_fusion.2 = bf16[1024,896]{1,0:T(8,128)(2,1)S(1)} fusion(f32[1024,896]{1,0:T(8,128)S(1)} %fusion.9, bf16[1024,2048]{1,0:T(8,128)(2,1)S(1)} %copy-done.17, bf16[1,2048,896]{2,1,0:T(8,128)(2,1)S(1)} %copy-done.18), kind=kOutput, calls=%fused_computation.22 | convolution fusion | flops 3763601408 | bytes 13369344 | tf_op jit(solution)/shard_map/dot_general | solution.py:150
  187.8 6.1 %convolution_convert_fusion.2 = bf16[1024,2048]{1,0:T(8,128)(2,1)} fusion(bf16[1024,896]{1,0:T(8,128)(2,1)S(1)} %multiply_convert_fusion.2, bf16[1,896,2048]{2,1,0:T(8,128)(2,1)S(1)} %copy-done.20), kind=kOutput, calls=%fused_computation.12 | convolution fusion | flops 3760193536 | bytes 9699328 | tf_op jit(solution)/shard_map/dot_general | solution.py:154
  194.3 17.3 %all-gather.3.cloned.1.call-done = bf16[1152,2048]{1,0:T(8,128)(2,1)} async-done(((bf16[144,2048]{1,0:T(8,128)(2,1)}), bf16[1152,2048]{1,0:T(8,128)(2,1)}) %all-gather.3.cloned.1.call-update) | async-done | bytes 4718608 | tf_op jit(solution)/shard_map/all_gather | solution.py:149
  211.5 8.1 %fusion.14 = f32[1152,896]{1,0:T(8,128)S(1)} fusion(bf16[1152,2048]{1,0:T(8,128)(2,1)} %all-gather.3.cloned.1.call-done, bf16[1,2048,896]{2,1,0:T(8,128)(2,1)} %param.28), kind=kOutput, calls=%fused_computation.20 | convolution fusion | flops 4227858432 | bytes 12517376 | tf_op jit(solution)/shard_map/dot_general | solution.py:150
  219.7 5.3 %fusion.16 = bf16[1152,896]{1,0:T(8,128)(2,1)S(1)} fusion(bf16[1152,2048]{1,0:T(8,128)(2,1)S(1)} %copy-done.16, bf16[1,2048,896]{2,1,0:T(8,128)(2,1)S(1)} %copy-done.19, f32[1152,896]{1,0:T(8,128)S(1)} %fusion.14), kind=kOutput, calls=%fused_computation.23 | convolution fusion | flops 4234051584 | bytes 14581760 | tf_op jit(solution)/shard_map/dot_general | solution.py:151
  225.0 6.7 %convolution_convert_fusion = bf16[1152,2048]{1,0:T(8,128)(2,1)} fusion(bf16[1152,896]{1,0:T(8,128)(2,1)S(1)} %fusion.16, bf16[1,896,2048]{2,1,0:T(8,128)(2,1)S(1)} %copy-done.21), kind=kOutput, calls=%fused_computation.2 | convolution fusion | flops 4230217728 | bytes 10452992 | tf_op jit(solution)/shard_map/dot_general | solution.py:154
  232.5 19.2 %reduce-scatter.8.cloned.1.call-done = bf16[128,2048]{1,0:T(8,128)(2,1)} async-done(((bf16[1024,2048]{1,0:T(8,128)(2,1)}), bf16[128,2048]{1,0:T(8,128)(2,1)}) %reduce-scatter.8.cloned.1.call-update) | async-done | bytes 524304 | tf_op jit(solution)/shard_map/reduce_scatter | solution.py:153
  251.8 6.9 %all-to-all-start.5 = ((bf16[16,8,2048]{2,1,0:T(8,128)(2,1)}), bf16[16,8,2048]{2,1,0:T(8,128)(2,1)S(1)}, u32[]{:S(2)}, u32[]{:S(2)}) async-start(bf16[16,8,2048]{2,1,0:T(8,128)(2,1)} %bitcast.209), calls=%async_computation.8 | async-start | bytes 1048576 | tf_op jit(solution)/shard_map/all_to_all | solution.py:160
  261.3 30.7 %reduce-scatter.6.cloned.1.call-done = bf16[144,2048]{1,0:T(8,128)(2,1)} async-done(((bf16[1152,2048]{1,0:T(8,128)(2,1)}), bf16[144,2048]{1,0:T(8,128)(2,1)}) %reduce-scatter.6.cloned.1.call-update) | async-done | bytes 589840 | tf_op jit(solution)/shard_map/reduce_scatter | solution.py:153
  291.9 2.3 reshape.1409
  294.2 7.2 %all-to-all-start.3 = ((bf16[16,9,2048]{2,1,0:T(8,128)(2,1)}), bf16[16,9,2048]{2,1,0:T(8,128)(2,1)S(1)}, u32[]{:S(2)}, u32[]{:S(2)}) async-start(bf16[16,9,2048]{2,1,0:T(8,128)(2,1)} %reshape.1409), calls=%async_computation.5 | async-start | bytes 2097152 | tf_op jit(solution)/shard_map/all_to_all | solution.py:160
  304.0 11.6 %all-to-all-done.3 = bf16[16,9,2048]{2,1,0:T(8,128)(2,1)S(1)} async-done(((bf16[16,9,2048]{2,1,0:T(8,128)(2,1)}), bf16[16,9,2048]{2,1,0:T(8,128)(2,1)S(1)}, u32[]{:S(2)}, u32[]{:S(2)}) %all-to-all-start.3) | async-done | bytes 589856 | tf_op jit(solution)/shard_map/all_to_all | solution.py:160
  315.6 1.5 pad_maximum_fusion
  317.2 1.6 reshape.1413
  318.8 2.3 gather_fusion
  321.1 1.7 gather.7
  322.9 4.1 %multiply_reduce_fusion = f32[128,2048]{1,0:T(8,128)S(1)} fusion(bf16[128,2,2048]{2,1,0:T(2,128)(2,1)S(1)} %gather.7, pred[128,2]{1,0:T(8,128)(4,1)S(1)} %copy.100, f32[128,2]{1,0:T(8,128)S(1)} %bitcast.210), kind=kLoop, calls=%fused_computation.35 | loop fusion | flops 1835008 | bytes 2098432 | tf_op jit(solution)/shard_map/reduce_sum | solution.py:170
  327.0 1.4 fusion.56
  331.4 1.2 fusion.30
  333.1 1.1 reshape.1414
  (150 shorter events, 28.0 us)
Async XLA Ops:
  6.5 78.5 %copy-start = (bf16[512,2048]{1,0:T(8,128)(2,1)S(1)}, bf16[512,2048]{1,0:T(8,128)(2,1)}, u32[]{:S(2)}) copy-start(bf16[512,2048]{1,0:T(8,128)(2,1)} %param.25) | copy-start | bytes 6291460
  6.5 8.0 %copy-start.9 = (f32[8,2,512]{2,1,0:T(2,128)S(1)}, f32[8,2,512]{2,1,0:T(2,128)}, u32[]{:S(2)}) copy-start(f32[8,2,512]{2,1,0:T(2,128)} %param.21) | copy-start | bytes 98308
  6.5 11.2 %copy-start.5 = (bf16[512,2,128]{2,1,0:T(2,128)(2,1)S(1)}, bf16[512,2,128]{2,1,0:T(2,128)(2,1)}, u32[]{:S(2)}) copy-start(bf16[512,2,128]{2,1,0:T(2,128)(2,1)} %param.19) | copy-start | bytes 786436
  18.2 1.0 copy-start.2
  19.2 14.1 %copy-start.15 = (f32[8]{0:T(128)S(1)}, f32[8]{0:T(128)}, u32[]{:S(2)}) copy-start(f32[8]{0:T(128)} %param.23) | copy-start | bytes 100
  20.4 16.8 %all-to-all-start = ((bf16[16,72,128]{2,1,0:T(8,128)(2,1)}), bf16[16,72,128]{2,1,0:T(8,128)(2,1)S(1)}, u32[]{:S(2)}, u32[]{:S(2)}) async-start(bf16[16,72,128]{2,1,0:T(8,128)(2,1)} %pad_maximum_fusion.1), calls=%async_computation | async-start | bytes 589824 | tf_op jit(solution)/shard_map/all_to_all | solution.py:84
  38.5 24.6 %copy-start.8 = (f32[2,256,2,8]{1,3,2,0:T(8,128)S(1)}, f32[2,256,2,8]{1,3,2,0:T(8,128)}, u32[]{:S(2)}) copy-start(f32[2,256,2,8]{1,3,2,0:T(8,128)} %get-tuple-element.11) | copy-start | bytes 98308
  38.5 24.6 %copy-start.10 = (f32[8,2,2,256]{3,0,1,2:T(8,128)S(1)}, f32[8,2,2,256]{3,0,1,2:T(8,128)}, u32[]{:S(2)}) copy-start(f32[8,2,2,256]{3,0,1,2:T(8,128)} %copy.132) | copy-start | bytes 98308
  46.4 14.4 %all-to-all-start.1 = ((bf16[16,64,128]{2,1,0:T(8,128)(2,1)}), bf16[16,64,128]{2,1,0:T(8,128)(2,1)S(1)}, u32[]{:S(2)}, u32[]{:S(2)}) async-start(bf16[16,64,128]{2,1,0:T(8,128)(2,1)} %constant_dynamic-update-slice_fusion), calls=%async_computation.1 | async-start | bytes 524288 | tf_op jit(solution)/shard_map/all_to_all | solution.py:94
  52.2 74.9 %reduce-scatter.4.cloned.1.call-start = ((), (), s32[]{:S(2)}) async-start(), calls=%async_computation.9 | async-start | bytes 4718592 | tf_op jit(solution)/shard_map/reduce_scatter | solution.py:118
  60.7 2.4 copy-start.3
  60.7 2.4 copy-start.4
  60.7 2.4 copy-start.11
  77.2 7.8 %copy-start.22 = (f32[512]{0:T(512)S(1)}, f32[512]{0:T(512)}, u32[]{:S(2)}) copy-start(f32[512]{0:T(512)} %param.24) | copy-start | bytes 6148
  90.9 0.7 copy-start.13
  90.9 2.7 copy-start.6
  90.9 37.4 %copy-start.12 = (f32[2048]{0:T(1024)S(1)}, f32[2048]{0:T(1024)}, u32[]{:S(2)}) copy-start(f32[2048]{0:T(1024)} %param.27) | copy-start | bytes 24580
  91.0 84.6 %all-gather.5.cloned.1.call-start = ((), (), s32[]{:S(2)}) async-start(), calls=%async_computation.12 | async-start | bytes 4718592 | tf_op jit(solution)/shard_map/all_gather | solution.py:149
  146.9 64.7 %all-gather.3.cloned.1.call-start = ((), (), s32[]{:S(2)}) async-start(), calls=%async_computation.10 | async-start | bytes 5308416 | tf_op jit(solution)/shard_map/all_gather | solution.py:149
  165.1 86.7 %reduce-scatter.8.cloned.1.call-start = ((), (), s32[]{:S(2)}) async-start(), calls=%async_computation.13 | async-start | bytes 4718592 | tf_op jit(solution)/shard_map/reduce_scatter | solution.py:153
  175.5 7.5 %copy-start.17 = (bf16[1024,2048]{1,0:T(8,128)(2,1)S(1)}, bf16[1024,2048]{1,0:T(8,128)(2,1)}, u32[]{:S(2)}) copy-start(bf16[1024,2048]{1,0:T(8,128)(2,1)} %all-gather.5.cloned.1.call-done) | copy-start | bytes 12582916
  175.5 7.5 %copy-start.18 = (bf16[1,2048,896]{2,1,0:T(8,128)(2,1)S(1)}, bf16[1,2048,896]{2,1,0:T(8,128)(2,1)}, u32[]{:S(2)}) copy-start(bf16[1,2048,896]{2,1,0:T(8,128)(2,1)} %param.28) | copy-start | bytes 11010052
  183.1 4.8 %copy-start.20 = (bf16[1,896,2048]{2,1,0:T(8,128)(2,1)S(1)}, bf16[1,896,2048]{2,1,0:T(8,128)(2,1)}, u32[]{:S(2)}) copy-start(bf16[1,896,2048]{2,1,0:T(8,128)(2,1)} %param.30) | copy-start | bytes 11010052
  194.0 98.0 %reduce-scatter.6.cloned.1.call-start = ((), (), s32[]{:S(2)}) async-start(), calls=%async_computation.11 | async-start | bytes 5308416 | tf_op jit(solution)/shard_map/reduce_scatter | solution.py:153
  211.5 8.1 %copy-start.16 = (bf16[1152,2048]{1,0:T(8,128)(2,1)S(1)}, bf16[1152,2048]{1,0:T(8,128)(2,1)}, u32[]{:S(2)}) copy-start(bf16[1152,2048]{1,0:T(8,128)(2,1)} %all-gather.3.cloned.1.call-done) | copy-start | bytes 14155780
  211.5 8.1 %copy-start.19 = (bf16[1,2048,896]{2,1,0:T(8,128)(2,1)S(1)}, bf16[1,2048,896]{2,1,0:T(8,128)(2,1)}, u32[]{:S(2)}) copy-start(bf16[1,2048,896]{2,1,0:T(8,128)(2,1)} %param.29) | copy-start | bytes 11010052
  219.7 5.3 %copy-start.21 = (bf16[1,896,2048]{2,1,0:T(8,128)(2,1)S(1)}, bf16[1,896,2048]{2,1,0:T(8,128)(2,1)}, u32[]{:S(2)}) copy-start(bf16[1,896,2048]{2,1,0:T(8,128)(2,1)} %param.30) | copy-start | bytes 11010052
  231.7 0.7 copy-start.14
  231.7 27.0 %copy-start.7 = (f32[4,2048]{1,0:T(4,128)S(1)}, f32[4,2048]{1,0:T(4,128)}, u32[]{:S(2)}) copy-start(f32[4,2048]{1,0:T(4,128)} %param.33) | copy-start | bytes 98308
  251.8 42.5 %all-to-all-start.5 = ((bf16[16,8,2048]{2,1,0:T(8,128)(2,1)}), bf16[16,8,2048]{2,1,0:T(8,128)(2,1)S(1)}, u32[]{:S(2)}, u32[]{:S(2)}) async-start(bf16[16,8,2048]{2,1,0:T(8,128)(2,1)} %bitcast.209), calls=%async_computation.8 | async-start | bytes 1048576 | tf_op jit(solution)/shard_map/all_to_all | solution.py:160
  294.2 21.4 %all-to-all-start.3 = ((bf16[16,9,2048]{2,1,0:T(8,128)(2,1)}), bf16[16,9,2048]{2,1,0:T(8,128)(2,1)S(1)}, u32[]{:S(2)}, u32[]{:S(2)}) async-start(bf16[16,9,2048]{2,1,0:T(8,128)(2,1)} %reshape.1409), calls=%async_computation.5 | async-start | bytes 2097152 | tf_op jit(solution)/shard_map/all_to_all | solution.py:160
  326.9 7.3 %copy-start.1 = (bf16[512,2048]{1,0:T(8,128)(2,1)S(1)}, bf16[512,2048]{1,0:T(8,128)(2,1)}, u32[]{:S(2)}) copy-start(bf16[512,2048]{1,0:T(8,128)(2,1)} %param.25) | copy-start | bytes 6291460
Sparse Core Ops, SparseCore 0:
  91.1 35.9 reduce-scatter.3
  147.0 28.5 all-gather.4
  177.2 34.2 all-gather.2
  213.8 37.9 reduce-scatter.7
  254.0 37.8 reduce-scatter.5
